TPU v7x, 512 devices: a whole 4x8x8 slice. The times are simulated.
512 devices in a mesh: rows: 8 (over y), mp: 64 (over z, x, core).
Axes of the slice: x: 4, y: 8, z: 8, core: 2. Of those that a mesh axis runs over, the one named last changes fastest.
Arguments:
- lam_out: bfloat16 [1024, 64, 1024], P('mp', 'rows'), may hold values from -6 to 6
- q_down: bfloat16 [1024, 4096], P(None, 'rows'), may hold values from -127 to 127, as said below
- down_scale: float32 [1024], replicated, may hold values from 0.0001 to 0.001
- q_up: bfloat16 [4096, 1024], P('rows'), may hold values from -127 to 127, as said below
- up_scale: float32 [4096], P('rows'), may hold values from 5e-05 to 0.0005
- chan_slopes: bfloat16 [2, 1024, 8, 4096], P(None, 'mp', 'rows'), may hold values from -0.14941406 to 1.09375
- chan_icpt: bfloat16 [2, 1024, 8, 4096], P(None, 'mp', 'rows')
- tok_in_blocks: bfloat16 [16, 128, 128], replicated, may hold values from -0.25 to 0.25
- tok_out_blocks: bfloat16 [16, 128, 128], replicated, may hold values from -0.25 to 0.25
- block_cells: int32 [16], replicated, may hold values from 0 to 31, as said below
- tok_slopes: bfloat16 [2, 512, 8, 1024], P(None, None, 'rows', 'mp'), may hold values from -0.14941406 to 1.09375
- tok_icpt: bfloat16 [2, 512, 8, 1024], P(None, None, 'rows', 'mp')
Outputs:
- lam_in: bfloat16 [1024, 64, 1024], P(None, 'rows', 'mp')
- bias: float32 [64], P('rows')
Inputs may be any that keep to these rules, and one draw needn't show every extreme that they name: `q_down`: integer values, 8-bit signed codes; a program may carry them across devices in any exact packed form, several codes to an element. `q_up`: integer values, 8-bit signed codes; a program may carry them across devices in any exact packed form, several codes to an element. `block_cells`: 16 distinct cells; cell h * 8 + u is hidden block h and token block u.
All inputs are finite; a program needn't handle non-finite values.
Results may differ from a plain program's by a relative error of at most 0.012.
Values may be sent and summed in bfloat16 or wider, within the bound.
No kernel may reach another device: no remote copies, remote signals or barrier semaphores. Data moves between devices by JAX's collectives and lax.ppermute only.
A program may use at most 64 MiB of HBM per device.

v0:
```python
import jax
import jax.numpy as jnp
from jax import lax
from jax.sharding import PartitionSpec as P

D = 1024
CH = 4096
TH = 512
TOK = 1024
BLK = 128
SPEC = 8
IMG_DEV = 1
NHB = 4
NTB = 8


def dense_blocks(blocks, cells, count_rows, count_cols):
    row_hot = (
        cells[:, None] // count_cols == jnp.arange(count_rows, dtype=jnp.int32)[None, :]
    ).astype(jnp.float32)
    col_hot = (
        cells[:, None] % count_cols == jnp.arange(count_cols, dtype=jnp.int32)[None, :]
    ).astype(jnp.float32)
    dense = jnp.einsum("bh,bt,bij->hitj", row_hot, col_hot, blocks.astype(jnp.float32))
    return dense.reshape(count_rows * BLK, count_cols * BLK).astype(jnp.bfloat16)


def relax(pre, slopes, icpt):
    pos = jnp.maximum(pre, 0.0)
    neg = jnp.minimum(pre, 0.0)
    lower = slopes[0].astype(jnp.float32)[:, :, None, :]
    upper = slopes[1].astype(jnp.float32)[:, :, None, :]
    icpt_low = icpt[0].astype(jnp.float32)[:, :, None, :]
    icpt_high = icpt[1].astype(jnp.float32)[:, :, None, :]
    mid = pos * lower + neg * upper
    row_bias = jnp.sum(pos * icpt_low + neg * icpt_high, axis=(0, 3)).reshape(-1)
    return (mid, row_bias)


def on_device(
    lam_out,
    q_down,
    down_scale,
    q_up,
    up_scale,
    chan_slopes,
    chan_icpt,
    tok_in_blocks,
    tok_out_blocks,
    block_cells,
    tok_slopes,
    tok_icpt,
):
    tok_dev = lam_out.shape[0]
    rows_dev = lam_out.shape[1]
    rows_all = rows_dev * lax.axis_size("rows")
    offset = lax.axis_index("rows") * rows_dev
    scaled = (lam_out.astype(jnp.float32) * down_scale).astype(jnp.bfloat16)
    flat = scaled.reshape(-1, D)
    pre = jnp.dot(
        flat, lax.all_gather(q_down, "rows", axis=1, tiled=True), preferred_element_type=jnp.float32
    )
    pre = pre.reshape(tok_dev, IMG_DEV, SPEC, CH)
    mid, own_bias = relax(pre, chan_slopes, chan_icpt)
    mid_flat = mid.reshape(-1, CH)
    codes = lax.all_gather(q_up, "rows", axis=0, tiled=True)
    scales = lax.all_gather(up_scale.astype(jnp.bfloat16), "rows", axis=0, tiled=True).astype(
        jnp.float32
    )
    weighted = (mid_flat * scales).astype(jnp.bfloat16)
    summed = jnp.dot(weighted, codes, preferred_element_type=jnp.float32)
    summed = summed.reshape(tok_dev, rows_dev, D)
    chan_bias = lax.dynamic_update_slice_in_dim(
        jnp.zeros((rows_all,), jnp.float32), own_bias, offset, 0
    )
    lam_res = (lam_out.astype(jnp.float32) + summed).astype(jnp.bfloat16)
    turned = lax.all_to_all(lam_res, "mp", split_axis=2, concat_axis=0, tiled=True)
    chan_dev = turned.shape[2]
    columns = turned.reshape(TOK, rows_dev * chan_dev)
    tok_in = dense_blocks(tok_in_blocks, block_cells, NHB, NTB)
    swapped = block_cells % NTB * NHB + block_cells // NTB
    tok_out = dense_blocks(tok_out_blocks, swapped, NTB, NHB)
    tpre = lax.dot_general(
        tok_out, columns, (((0,), (0,)), ((), ())), preferred_element_type=jnp.float32
    )
    tpre = tpre.reshape(TH, IMG_DEV, SPEC, chan_dev)
    tmid, tok_bias = relax(tpre, tok_slopes, tok_icpt)
    tmid = tmid.astype(jnp.bfloat16).reshape(TH, rows_dev * chan_dev)
    back = lax.dot_general(
        tok_in, tmid, (((0,), (0,)), ((), ())), preferred_element_type=jnp.float32
    )
    lam_in = (turned.astype(jnp.float32) + back.reshape(TOK, rows_dev, chan_dev)).astype(
        jnp.bfloat16
    )
    placed = lax.dynamic_update_slice_in_dim(
        jnp.zeros((rows_all,), jnp.float32), tok_bias, offset, 0
    )
    totals = lax.psum(chan_bias + placed, ("rows", "mp"))
    bias = lax.dynamic_slice_in_dim(totals, offset, rows_dev, 0)
    return (lam_in, bias)


def solution(mesh):
    return jax.shard_map(
        on_device,
        mesh=mesh,
        in_specs=(
            P("mp", "rows", None),
            P(None, "rows"),
            P(),
            P("rows", None),
            P("rows"),
            P(None, "mp", "rows", None),
            P(None, "mp", "rows", None),
            P(),
            P(),
            P(),
            P(None, None, "rows", "mp"),
            P(None, None, "rows", "mp"),
        ),
        out_specs=(P(None, "rows", "mp"), P("rows")),
        check_vma=False,
    )
```

profile of v0, /device:TPU:1, one launch (start us, length us, event | category | flops | bytes accessed | tf_op | source)
XLA Modules:
  0.0 366.1 jit_solution(10095562536390558608)
XLA Ops:
  7.2 0.0 copy-start.9
  7.2 0.0 copy-start.10
  7.2 0.0 copy-start.2
  7.2 0.0 copy-start.4
  7.2 0.0 copy-start.5
  7.2 0.0 all-gather.4.cloned.1.call-start
  7.3 0.7 all-gather.4.cloned.1.call-update
  8.0 0.0 copy-start.1
  8.0 0.0 copy-start.8
  8.0 0.0 all-gather.6.cloned.1.call-start
  8.0 0.7 all-gather.6.cloned.1.call-update
  8.7 0.0 copy-done.9
  8.8 19.1 %all-gather = bf16[8,1,512]{2,1,0:T(2,128)(2,1)S(1)} all-gather(bf16[1,1,512]{2,1,0:T(2,128)(2,1)S(1)} %reshape.231), channel_id=1, replica_groups=mesh['rows'=8,'mp'=64] {'rows'}, dimensions={0}, use_global_device_ids=true | all-gather | bytes 9216 | tf_op jit(solution)/shard_map/all_gather | solution.py:67
  28.0 1.4 fusion.8
  29.4 0.0 copy-done.5
  29.5 82.6 %all-gather.4.cloned.1.call-done = bf16[1024,4096]{1,0:T(8,128)(2,1)} async-done(((bf16[1024,512]{1,0:T(8,128)(2,1)}), bf16[1024,4096]{1,0:T(8,128)(2,1)}) %all-gather.4.cloned.1.call-update) | async-done | bytes 8388624 | tf_op jit(solution)/shard_map/all_gather | solution.py:61
  112.1 0.0 copy-done.8
  112.1 5.1 %fusion.3 = (f32[128]{0:T(128)S(1)}, f32[128,4096]{1,0:T(8,128)S(1)}) fusion(f32[16,4096]{1,0:T(8,128)S(1)} %get-tuple-element.9, f32[16,4096]{1,0:T(8,128)S(1)} %get-tuple-element.8, bf16[1024,4096]{1,0:T(8,128)(2,1)} %all-gather.4.cloned.1.call-done, bf16[16,8,1024]{2,1,0:T(8,128)(2,1)S(1)} %copy-done.1, f32[1024]{0:T(1024)S(1)} %copy-done.8), kind=kOutput, calls=%fused_computation.4 | convolution fusion | flops 1077280640 | bytes 11276800 | tf_op jit(solution)/shard_map/dot_general | solution.py:60
  117.2 92.5 %all-gather.6.cloned.1.call-done = bf16[4096,1024]{1,0:T(8,128)(2,1)} async-done(((bf16[512,1024]{1,0:T(8,128)(2,1)}), bf16[4096,1024]{1,0:T(8,128)(2,1)}) %all-gather.6.cloned.1.call-update) | async-done | bytes 8388624 | tf_op jit(solution)/shard_map/all_gather | solution.py:66
  209.7 4.8 %fusion.12 = bf16[16,8,1024]{2,1,0:T(8,128)(2,1)S(1)} fusion(bf16[4096,1024]{1,0:T(8,128)(2,1)} %all-gather.6.cloned.1.call-done, f32[128,4096]{1,0:T(8,128)S(1)} %get-tuple-element.17, f32[4096]{0:T(1024)S(1)} %bitcast.143, f32[16,4096]{1,0:T(8,128)S(1)} %get-tuple-element.11, f32[16,4096]{1,0:T(8,128)S(1)} %get-tuple-element.10, ...), kind=kOutput, calls=%fused_computation.17 | convolution fusion | flops 1077805056 | bytes 11550720 | tf_op jit(solution)/shard_map/dot_general | solution.py:71
  214.6 1.7 copy.36
  216.3 2.9 reshape.241
  219.2 11.2 %all-to-all-start = ((bf16[64,2,1024]{2,1,0:T(2,128)(2,1)}), bf16[64,2,1024]{2,1,0:T(2,128)(2,1)S(1)}, u32[]{:S(2)}, u32[]{:S(2)}) async-start(bf16[64,2,1024]{2,1,0:T(2,128)(2,1)} %reshape.241), calls=%async_computation | async-start | bytes 524288 | tf_op jit(solution)/shard_map/all_to_all | solution.py:77
  230.4 2.0 copy.42
  232.3 0.0 copy-start.6
  232.4 0.0 copy-start.7
  232.4 0.5 fusion.7
  232.9 1.3 reshape.239
  234.1 0.0 copy-done.7
  234.1 0.7 bitcast_convert_fusion.6
  234.8 0.1 reduce_sum.24
  234.9 0.2 dynamic_update_slice.8
  235.2 8.4 %all-to-all-done = bf16[64,2,1024]{2,1,0:T(2,128)(2,1)S(1)} async-done(((bf16[64,2,1024]{2,1,0:T(2,128)(2,1)}), bf16[64,2,1024]{2,1,0:T(2,128)(2,1)S(1)}, u32[]{:S(2)}, u32[]{:S(2)}) %all-to-all-start) | async-done | bytes 262176 | tf_op jit(solution)/shard_map/all_to_all | solution.py:77
  243.5 1.4 reshape.242
  245.0 3.4 copy.43
  248.4 3.0 reshape.221
  251.4 1.4 fusion.34
  252.8 0.1 reduce_sum.36
  252.9 0.1 reduce_sum.37
  253.0 0.2 add_dynamic-update-slice_fusion
  253.2 94.2 %psum.7 = f32[64]{0:T(128)S(1)} all-reduce(f32[64]{0:T(128)S(1)} %add_dynamic-update-slice_fusion), channel_id=1, replica_groups=mesh['rows'=8,'mp'=64] {'rows','mp'}, use_global_device_ids=true, to_apply=%region_4.5 | all-reduce | flops 64 | bytes 512 | tf_op jit(solution)/shard_map/psum | solution.py:98
  347.4 0.6 dynamic_slice.3
  348.0 2.6 copy.38
  350.6 0.1 bitcast_convert_fusion
  350.7 2.7 copy.39
  353.4 4.8 %reshape.224 = f32[1024,8,16]{0,2,1:T(8,128)S(1)} reshape(f32[64,16,8,16]{1,0,3,2:T(8,128)} %copy.39) | data formatting | bytes 1048576 | tf_op jit(solution)/shard_map/convert_element_type | solution.py:92
  358.2 0.0 copy-done
  358.2 1.0 fusion.15
  (20 shorter events, 0.2 us)
Async XLA Ops:
  7.2 1.6 copy-start.9
  7.2 20.7 %copy-start.10 = (s32[16]{0:T(128)S(1)}, s32[16]{0:T(128)}, u32[]{:S(2)}) copy-start(s32[16]{0:T(128)} %param.21) | copy-start | bytes 196
  7.2 20.8 %copy-start.2 = (bf16[16,128,128]{2,1,0:T(8,128)(2,1)S(1)}, bf16[16,128,128]{2,1,0:T(8,128)(2,1)}, u32[]{:S(2)}) copy-start(bf16[16,128,128]{2,1,0:T(8,128)(2,1)} %param.20) | copy-start | bytes 1572868
  7.2 22.2 %copy-start.4 = (bf16[2,16,1,4096]{3,1,2,0:T(8,128)(2,1)S(1)}, bf16[2,16,1,4096]{3,1,2,0:T(8,128)(2,1)}, u32[]{:S(2)}) copy-start(bf16[2,16,1,4096]{3,1,2,0:T(8,128)(2,1)} %param.18) | copy-start | bytes 786436
  7.2 22.2 %copy-start.5 = (bf16[2,16,1,4096]{3,1,2,0:T(8,128)(2,1)S(1)}, bf16[2,16,1,4096]{3,1,2,0:T(8,128)(2,1)}, u32[]{:S(2)}) copy-start(bf16[2,16,1,4096]{3,1,2,0:T(8,128)(2,1)} %param.17) | copy-start | bytes 786436
  7.2 104.9 %all-gather.4.cloned.1.call-start = ((), (), s32[]{:S(2)}) async-start(), calls=%async_computation.1 | async-start | bytes 9437184 | tf_op jit(solution)/shard_map/all_gather | solution.py:61
  8.0 104.2 %copy-start.1 = (bf16[16,8,1024]{2,1,0:T(8,128)(2,1)S(1)}, bf16[16,8,1024]{2,1,0:T(8,128)(2,1)}, u32[]{:S(2)}) copy-start(bf16[16,8,1024]{2,1,0:T(8,128)(2,1)} %param.12) | copy-start | bytes 786436
  8.0 104.1 %copy-start.8 = (f32[1024]{0:T(1024)S(1)}, f32[1024]{0:T(1024)}, u32[]{:S(2)}) copy-start(f32[1024]{0:T(1024)} %param.14) | copy-start | bytes 12292
  8.0 201.8 %all-gather.6.cloned.1.call-start = ((), (), s32[]{:S(2)}) async-start(), calls=%async_computation.2 | async-start | bytes 9437184 | tf_op jit(solution)/shard_map/all_gather | solution.py:66
  219.2 13.2 %copy-start.3 = (bf16[16,128,128]{2,1,0:T(8,128)(2,1)S(1)}, bf16[16,128,128]{2,1,0:T(8,128)(2,1)}, u32[]{:S(2)}) copy-start(bf16[16,128,128]{2,1,0:T(8,128)(2,1)} %param.19) | copy-start | bytes 1572868
  219.2 24.3 %all-to-all-start = ((bf16[64,2,1024]{2,1,0:T(2,128)(2,1)}), bf16[64,2,1024]{2,1,0:T(2,128)(2,1)S(1)}, u32[]{:S(2)}, u32[]{:S(2)}) async-start(bf16[64,2,1024]{2,1,0:T(2,128)(2,1)} %reshape.241), calls=%async_computation | async-start | bytes 524288 | tf_op jit(solution)/shard_map/all_to_all | solution.py:77
  232.3 1.8 copy-start.6
  232.4 1.8 copy-start.7
  353.4 4.8 %copy-start = (bf16[512,1024,1]{1,0,2:T(8,128)(2,1)S(1)}, bf16[512,1024,1]{1,0,2:T(8,128)(2,1)}, u32[]{:S(2)}) copy-start(bf16[512,1024,1]{1,0,2:T(8,128)(2,1)} %reshape.239) | copy-start | bytes 3145732
Sparse Core Ops, SparseCore 0:
  10.1 101.9 all-gather.3
  114.2 95.5 all-gather.5
where the time goes:
time: 367 us; the launch traced here: 366 us
  waiting for transfers between devices  185 us (50%)
  blocking collectives  113 us (31%)
  local copies, waits for them, and re-layouts  26.8 us (7%)
  matrix products  14.3 us (4%)
  between operations  14.3 us (4%)
  starting transfers between devices  11.2 us (3%)
    psum x1, blocking collectives, on_device(): totals = lax.psum(chan_bias + placed, ('rows', 'mp'))  94.2 us
    all_gather x1, waiting for transfers between devices, on_device(): codes = lax.all_gather(q_up, 'rows', axis=0, tiled=True)  92.5 us
    all_gather x1, waiting for transfers between devices, on_device(): lax.all_gather(q_down, 'rows', axis=1, tiled=True)  82.6 us
    all_gather x1, blocking collectives, on_device(): lax.all_gather(up_scale.astype(jnp.bfloat16), 'rows', axis=0, tiled=True)  19.1 us
    all_to_all x1, starting transfers between devices, on_device(): lax.all_to_all(lam_res, 'mp', split_axis=2, concat_axis=0, tiled=True)  11.2 us
    all_to_all x1, waiting for transfers between devices, on_device(): lax.all_to_all(lam_res, 'mp', split_axis=2, concat_axis=0, tiled=True)  8.38 us
    convert_element_type x2, local copies, waits for them, and re-layouts, on_device(): turned.astype(jnp.float32) + back.reshape(TOK, rows_dev, chan_dev)  7.48 us
  transfers between devices with their start and end apart: 3, of which 3 were waited for; matrix products, arithmetic and copies ran while one was open for 3% of the time, Pallas kernels for 0%

commit v1 on v0

--- a/solution.py
+++ b/solution.py
@@ -95,7 +95,7 @@
     placed = lax.dynamic_update_slice_in_dim(
         jnp.zeros((rows_all,), jnp.float32), tok_bias, offset, 0
     )
-    totals = lax.psum(chan_bias + placed, ("rows", "mp"))
+    totals = jnp.sum(lax.all_gather(chan_bias + placed, ("rows", "mp")), axis=0)
     bias = lax.dynamic_slice_in_dim(totals, offset, rows_dev, 0)
     return (lam_in, bias)
 

time: 367 us -> 333 us (0.907)
  blocking collectives: 113 us -> 78.9 us
    psum x1 -> x0, blocking collectives: 94.2 us -> none  [on_device(): totals = lax.psum(chan_bias + placed, ('rows', 'mp'))]
    all_gather x0 -> x1, blocking collectives: none -> 59.8 us  [on_device(): totals = jnp.sum(lax.all_gather(chan_bias + placed, ('rows', 'mp')), axis=0)]
where the time goes in v1:
time: 333 us; the launch traced here: 332 us
  waiting for transfers between devices  185 us (56%)
  blocking collectives  78.9 us (24%)
  local copies, waits for them, and re-layouts  26.9 us (8%)
  matrix products  14.3 us (4%)
  between operations  14.3 us (4%)
  starting transfers between devices  11.2 us (3%)
    all_gather x1, waiting for transfers between devices, on_device(): codes = lax.all_gather(q_up, 'rows', axis=0, tiled=True)  92.5 us
    all_gather x1, waiting for transfers between devices, on_device(): lax.all_gather(q_down, 'rows', axis=1, tiled=True)  82.6 us
    all_gather x1, blocking collectives, on_device(): totals = jnp.sum(lax.all_gather(chan_bias + placed, ('rows', 'mp')), axis=0)  59.8 us
    all_gather x1, blocking collectives, on_device(): lax.all_gather(up_scale.astype(jnp.bfloat16), 'rows', axis=0, tiled=True)  19.1 us
    all_to_all x1, starting transfers between devices, on_device(): lax.all_to_all(lam_res, 'mp', split_axis=2, concat_axis=0, tiled=True)  11.2 us
    all_to_all x1, waiting for transfers between devices, on_device(): lax.all_to_all(lam_res, 'mp', split_axis=2, concat_axis=0, tiled=True)  8.38 us
    convert_element_type x2, local copies, waits for them, and re-layouts, on_device(): turned.astype(jnp.float32) + back.reshape(TOK, rows_dev, chan_dev)  7.48 us
  transfers between devices with their start and end apart: 3, of which 3 were waited for; matrix products, arithmetic and copies ran while one was open for 3% of the time, Pallas kernels for 0%

profile of v1, /device:TPU:1, one launch (start us, length us, event | category | flops | bytes accessed | tf_op | source)
XLA Modules:
  0.0 332.2 jit_solution(11545687900193346057)
XLA Ops:
  7.2 0.0 copy-start.9
  7.2 0.0 copy-start.10
  7.2 0.0 copy-start.2
  7.2 0.0 copy-start.4
  7.2 0.0 copy-start.5
  7.2 0.0 all-gather.5.cloned.1.call-start
  7.3 0.7 all-gather.5.cloned.1.call-update
  8.0 0.0 copy-start.1
  8.0 0.0 copy-start.8
  8.0 0.0 all-gather.7.cloned.1.call-start
  8.0 0.7 all-gather.7.cloned.1.call-update
  8.8 19.1 %all-gather = bf16[8,1,512]{2,1,0:T(2,128)(2,1)S(1)} all-gather(bf16[1,1,512]{2,1,0:T(2,128)(2,1)S(1)} %reshape.233), channel_id=1, replica_groups=mesh['rows'=8,'mp'=64] {'rows'}, dimensions={0}, use_global_device_ids=true | all-gather | bytes 9216 | tf_op jit(solution)/shard_map/all_gather | solution.py:67
  28.0 1.4 fusion.8
  29.4 0.0 copy-done.5
  29.5 82.6 %all-gather.5.cloned.1.call-done = bf16[1024,4096]{1,0:T(8,128)(2,1)} async-done(((bf16[1024,512]{1,0:T(8,128)(2,1)}), bf16[1024,4096]{1,0:T(8,128)(2,1)}) %all-gather.5.cloned.1.call-update) | async-done | bytes 8388624 | tf_op jit(solution)/shard_map/all_gather | solution.py:61
  112.1 0.0 copy-done.8
  112.1 5.1 %fusion.3 = (f32[128]{0:T(128)S(1)}, f32[128,4096]{1,0:T(8,128)S(1)}) fusion(f32[16,4096]{1,0:T(8,128)S(1)} %get-tuple-element.9, f32[16,4096]{1,0:T(8,128)S(1)} %get-tuple-element.8, bf16[1024,4096]{1,0:T(8,128)(2,1)} %all-gather.5.cloned.1.call-done, bf16[16,8,1024]{2,1,0:T(8,128)(2,1)S(1)} %copy-done.1, f32[1024]{0:T(1024)S(1)} %copy-done.8), kind=kOutput, calls=%fused_computation.4 | convolution fusion | flops 1077280640 | bytes 11276800 | tf_op jit(solution)/shard_map/dot_general | solution.py:60
  117.2 92.5 %all-gather.7.cloned.1.call-done = bf16[4096,1024]{1,0:T(8,128)(2,1)} async-done(((bf16[512,1024]{1,0:T(8,128)(2,1)}), bf16[4096,1024]{1,0:T(8,128)(2,1)}) %all-gather.7.cloned.1.call-update) | async-done | bytes 8388624 | tf_op jit(solution)/shard_map/all_gather | solution.py:66
  209.7 4.8 %fusion.12 = bf16[16,8,1024]{2,1,0:T(8,128)(2,1)S(1)} fusion(bf16[4096,1024]{1,0:T(8,128)(2,1)} %all-gather.7.cloned.1.call-done, f32[128,4096]{1,0:T(8,128)S(1)} %get-tuple-element.17, f32[4096]{0:T(1024)S(1)} %bitcast.146, f32[16,4096]{1,0:T(8,128)S(1)} %get-tuple-element.11, f32[16,4096]{1,0:T(8,128)S(1)} %get-tuple-element.10, ...), kind=kOutput, calls=%fused_computation.17 | convolution fusion | flops 1077805056 | bytes 11550720 | tf_op jit(solution)/shard_map/dot_general | solution.py:71
  214.6 1.7 copy.36
  216.3 2.9 reshape.249
  219.2 11.2 %all-to-all-start = ((bf16[64,2,1024]{2,1,0:T(2,128)(2,1)}), bf16[64,2,1024]{2,1,0:T(2,128)(2,1)S(1)}, u32[]{:S(2)}, u32[]{:S(2)}) async-start(bf16[64,2,1024]{2,1,0:T(2,128)(2,1)} %reshape.249), calls=%async_computation | async-start | bytes 524288 | tf_op jit(solution)/shard_map/all_to_all | solution.py:77
  230.4 2.0 copy.42
  232.3 0.0 copy-start.6
  232.4 0.0 copy-start.7
  232.4 0.5 fusion.7
  232.9 1.3 reshape.247
  234.1 0.0 copy-done.7
  234.1 0.7 bitcast_convert_fusion.6
  234.8 0.1 reduce_sum.32
  234.9 0.2 dynamic_update_slice.8
  235.2 8.4 %all-to-all-done = bf16[64,2,1024]{2,1,0:T(2,128)(2,1)S(1)} async-done(((bf16[64,2,1024]{2,1,0:T(2,128)(2,1)}), bf16[64,2,1024]{2,1,0:T(2,128)(2,1)S(1)}, u32[]{:S(2)}, u32[]{:S(2)}) %all-to-all-start) | async-done | bytes 262176 | tf_op jit(solution)/shard_map/all_to_all | solution.py:77
  243.5 1.4 reshape.250
  245.0 3.4 %copy.43 = bf16[64,16,8,16]{3,2,1,0:T(8,128)(2,1)} copy(bf16[64,16,8,16]{1,2,3,0:T(8,128)(2,1)S(1)} %bitcast.142) | data formatting | bytes 524288 | tf_op jit(solution)/shard_map/all_to_all | solution.py:77
  248.4 3.0 reshape.223
  251.4 1.4 fusion.34
  252.8 0.1 reduce_sum.45
  252.9 0.1 reduce_sum.46
  253.0 0.1 add_bitcast_fusion
  253.1 0.1 add.74
  253.2 59.8 %all-gather.1 = f32[512,1,64]{2,1,0:T(1,128)S(1)} all-gather(f32[1,1,64]{2,1,0:T(1,128)S(1)} %add.74), channel_id=1, replica_groups=mesh['rows'=8,'mp'=64] {'rows','mp'}, dimensions={0}, use_global_device_ids=true | all-gather | bytes 131328 | tf_op jit(solution)/shard_map/all_gather | solution.py:98
  313.0 0.6 reduce_sum.47
  313.5 0.6 dynamic_slice.3
  314.1 2.6 copy.38
  316.7 0.1 bitcast_convert_fusion
  316.8 2.7 copy.39
  319.5 4.8 %reshape.226 = f32[1024,8,16]{0,2,1:T(8,128)S(1)} reshape(f32[64,16,8,16]{1,0,3,2:T(8,128)} %copy.39) | data formatting | bytes 1048576 | tf_op jit(solution)/shard_map/convert_element_type | solution.py:92
  324.3 1.0 fusion.15
  (22 shorter events, 0.2 us)
Async XLA Ops:
  7.2 1.6 copy-start.9
  7.2 20.7 %copy-start.10 = (s32[16]{0:T(128)S(1)}, s32[16]{0:T(128)}, u32[]{:S(2)}) copy-start(s32[16]{0:T(128)} %param.21) | copy-start | bytes 196
  7.2 20.8 %copy-start.2 = (bf16[16,128,128]{2,1,0:T(8,128)(2,1)S(1)}, bf16[16,128,128]{2,1,0:T(8,128)(2,1)}, u32[]{:S(2)}) copy-start(bf16[16,128,128]{2,1,0:T(8,128)(2,1)} %param.20) | copy-start | bytes 1572868
  7.2 22.2 %copy-start.4 = (bf16[2,16,1,4096]{3,1,2,0:T(8,128)(2,1)S(1)}, bf16[2,16,1,4096]{3,1,2,0:T(8,128)(2,1)}, u32[]{:S(2)}) copy-start(bf16[2,16,1,4096]{3,1,2,0:T(8,128)(2,1)} %param.18) | copy-start | bytes 786436
  7.2 22.2 %copy-start.5 = (bf16[2,16,1,4096]{3,1,2,0:T(8,128)(2,1)S(1)}, bf16[2,16,1,4096]{3,1,2,0:T(8,128)(2,1)}, u32[]{:S(2)}) copy-start(bf16[2,16,1,4096]{3,1,2,0:T(8,128)(2,1)} %param.17) | copy-start | bytes 786436
  7.2 104.9 %all-gather.5.cloned.1.call-start = ((), (), s32[]{:S(2)}) async-start(), calls=%async_computation.1 | async-start | bytes 9437184 | tf_op jit(solution)/shard_map/all_gather | solution.py:61
  8.0 104.2 %copy-start.1 = (bf16[16,8,1024]{2,1,0:T(8,128)(2,1)S(1)}, bf16[16,8,1024]{2,1,0:T(8,128)(2,1)}, u32[]{:S(2)}) copy-start(bf16[16,8,1024]{2,1,0:T(8,128)(2,1)} %param.12) | copy-start | bytes 786436
  8.0 104.1 %copy-start.8 = (f32[1024]{0:T(1024)S(1)}, f32[1024]{0:T(1024)}, u32[]{:S(2)}) copy-start(f32[1024]{0:T(1024)} %param.14) | copy-start | bytes 12292
  8.0 201.8 %all-gather.7.cloned.1.call-start = ((), (), s32[]{:S(2)}) async-start(), calls=%async_computation.2 | async-start | bytes 9437184 | tf_op jit(solution)/shard_map/all_gather | solution.py:66
  219.2 13.2 %copy-start.3 = (bf16[16,128,128]{2,1,0:T(8,128)(2,1)S(1)}, bf16[16,128,128]{2,1,0:T(8,128)(2,1)}, u32[]{:S(2)}) copy-start(bf16[16,128,128]{2,1,0:T(8,128)(2,1)} %param.19) | copy-start | bytes 1572868
  219.2 24.3 %all-to-all-start = ((bf16[64,2,1024]{2,1,0:T(2,128)(2,1)}), bf16[64,2,1024]{2,1,0:T(2,128)(2,1)S(1)}, u32[]{:S(2)}, u32[]{:S(2)}) async-start(bf16[64,2,1024]{2,1,0:T(2,128)(2,1)} %reshape.249), calls=%async_computation | async-start | bytes 524288 | tf_op jit(solution)/shard_map/all_to_all | solution.py:77
  232.3 1.8 copy-start.6
  232.4 1.8 copy-start.7
  319.5 4.8 %copy-start = (bf16[512,1024,1]{1,0,2:T(8,128)(2,1)S(1)}, bf16[512,1024,1]{1,0,2:T(8,128)(2,1)}, u32[]{:S(2)}) copy-start(bf16[512,1024,1]{1,0,2:T(8,128)(2,1)} %reshape.247) | copy-start | bytes 3145732
Sparse Core Ops, SparseCore 0:
  10.1 101.9 all-gather.4
  114.2 95.5 all-gather.6
